TPU v7x, 32 devices: a whole 2x2x4 slice. The times are simulated.
32 devices in a mesh: groups: 2 (over y), section: 2 (over x), shard: 8 (over z, core).
Axes of the slice: x: 2, y: 2, z: 4, core: 2. Of those that a mesh axis runs over, the one named last changes fastest.
Arguments:
- embed: bfloat16 [1024, 8192], P('groups', 'shard'), parts along dimension 0, may hold values from -6 to 6
- gains: float32 [4, 8192], P('section', 'shard'), may hold values from 0.25 to 1.75
- theta: float32 [4, 8, 2, 64, 8192], P('section', 'groups', None, None, 'shard'), parts along dimension 1, may hold values from -6 to 6
- iterate: float32 [4, 8, 2, 64, 8192], P('section', 'groups', None, None, 'shard'), parts along dimension 1, may hold values from -6 to 6
- residual: float32 [4, 8, 2, 64, 8192], P('section', 'groups', None, None, 'shard'), parts along dimension 1, may hold values from -6 to 6
- direction: float32 [4, 8, 2, 64, 8192], P('section', 'groups', None, None, 'shard'), parts along dimension 1, may hold values from -6 to 6
- token_task: int32 [1024], P('groups'), parts along dimension 0, may hold values from 0 to 3, never falling along the last dimension, each value on 1 to 256 neighbouring positions
- loss_mask: int32 [1024], P('groups'), parts along dimension 0, may hold values 0 or 1
Outputs:
- new_iterate: float32 [4, 8, 2, 64, 8192], P('section', 'groups', None, None, 'shard'), parts along dimension 1
- updated_residual_stream: float32 [4, 8, 2, 64, 8192], P('section', 'groups', None, None, 'shard'), parts along dimension 1
- new_direction: float32 [4, 8, 2, 64, 8192], P('section', 'groups', None, None, 'shard'), parts along dimension 1
There are 2 independent parts, one for each index of `groups`. A program takes and returns all parts, laid end to end along the dimension named above; an argument that names none is the same for every part. Nothing has to cross between parts.
Inputs may be any that keep to these rules, and one draw needn't show every extreme that they name: `token_task`: tokens of one task stand together, tasks in increasing order; each task has 1 to 256 tokens and one has exactly 256.
All inputs are finite; a program needn't handle non-finite values.
Results may differ from a plain program's by a relative error of at most 0.0003.
Values sent between devices are 32-bit elements; how exact they have to be, the bound alone decides.
A program may use at most 128 MiB of HBM per device.

v0:
```python
import jax
import jax.numpy as jnp
from jax import lax
from jax.sharding import PartitionSpec as P

D = 8192
ADAPTER_RANK = 64
MICRO = 2
EPSILON = 1e-05
ADAPTER_SCALE = 0.5
DAMPING_FACTOR = 0.5
HIGH = lax.Precision.HIGHEST


def shifted(value, axis, steps):
    count = lax.axis_size(axis)
    initial, last = (max(0, -steps), min(count, count - steps))
    return lax.ppermute(value, axis, [(source, source + steps) for source in range(initial, last)])


def pick_down(values, mats, onehot):
    expanded = jnp.einsum("td,krd->tkr", values, mats, precision=HIGH)
    return jnp.sum(expanded * onehot[:, :, None], axis=1)


def apply_up_projection(lowrank, mats, onehot):
    picked = onehot[:, :, None] * lowrank[:, None, :]
    return jnp.einsum("tkr,krd->td", picked, mats, precision=HIGH)


def task_outer(lowrank, values, onehot):
    picked = onehot[:, :, None] * lowrank[:, None, :]
    return jnp.einsum("tkr,td->krd", picked, values, precision=HIGH)


def keep_rows(store, value, layer_index, row_start, active):
    index = (jnp.int32(layer_index), row_start) + tuple((jnp.int32(0) for extra in value.shape[1:]))
    sizes = (1,) + value.shape
    previous = lax.dynamic_slice(store, index, sizes)[0]
    fresh = jnp.where(active, value, previous)
    return lax.dynamic_update_slice(store, fresh[None], index)


def layer_forward(hidden, moving, onehot, parameters, slope, gain_vector):
    down_scale = D ** (-0.5)
    up_projection_scale = ADAPTER_SCALE * ADAPTER_RANK ** (-0.5)
    scaled = hidden * gain_vector
    squares, products = lax.psum(
        (jnp.sum(hidden * hidden, axis=-1), jnp.sum(hidden * moving, axis=-1)), "shard"
    )
    recip = 1.0 / jnp.sqrt(squares / D + EPSILON)
    drift = -(recip**3) * products / D
    normed = scaled * recip[:, None]
    normed_move = gain_vector * (moving * recip[:, None] + hidden * drift[:, None])
    lowrank, lowmove = lax.psum(
        (
            pick_down(normed, parameters[:, 0], onehot) * down_scale,
            (
                pick_down(normed_move, parameters[:, 0], onehot)
                + pick_down(normed, slope[:, 0], onehot)
            )
            * down_scale,
        ),
        "shard",
    )
    result = hidden + up_projection_scale * apply_up_projection(lowrank, parameters[:, 1], onehot)
    result_move = moving + up_projection_scale * (
        apply_up_projection(lowmove, parameters[:, 1], onehot)
        + apply_up_projection(lowrank, slope[:, 1], onehot)
    )
    return (result, result_move, recip, lowrank)


def layer_backward(cotangent, hidden, recip, lowrank, onehot, parameters, gain_vector):
    down_scale = D ** (-0.5)
    up_projection_scale = ADAPTER_SCALE * ADAPTER_RANK ** (-0.5)
    grad_up = up_projection_scale * task_outer(lowrank, cotangent, onehot)
    partial_cot = up_projection_scale * pick_down(cotangent, parameters[:, 1], onehot)
    low_cot = lax.psum(partial_cot, "shard")
    normed = hidden * gain_vector * recip[:, None]
    grad_down = down_scale * task_outer(low_cot, normed, onehot)
    cot_norm = down_scale * apply_up_projection(low_cot, parameters[:, 0], onehot)
    row_total = lax.psum(jnp.sum(cot_norm * gain_vector * hidden, axis=-1), "shard")
    cot_input = (
        cotangent
        + gain_vector * cot_norm * recip[:, None]
        - (recip**3 * row_total / D)[:, None] * hidden
    )
    return (cot_input, jnp.stack([grad_down, grad_up], axis=1))


def body(embed, gains, theta, iterate, residual, direction, token_task, loss_mask):
    squared_old = lax.psum(jnp.sum(residual * residual), ("section", "shard"))
    section_index = lax.axis_index("section")
    sections = lax.axis_size("section")
    layers_here = theta.shape[0]
    tokens = embed.shape[0]
    width_here = embed.shape[1]
    lowrank_width = theta.shape[3]
    pieces = MICRO
    row_count = tokens // pieces
    onehot = (token_task[:, None] == jnp.arange(theta.shape[1], dtype=jnp.int32)[None, :]).astype(
        jnp.float32
    )
    weights = loss_mask.astype(jnp.float32)
    embedded = embed.astype(jnp.float32)
    saved_hidden = jnp.zeros((layers_here, tokens, width_here), jnp.float32)
    saved_recip = jnp.zeros((layers_here, tokens), jnp.float32)
    saved_low = jnp.zeros((layers_here, tokens, lowrank_width), jnp.float32)
    final_move = jnp.zeros((1, tokens, width_here), jnp.float32)
    incoming = jnp.zeros((row_count, width_here), jnp.float32)
    incoming_move = jnp.zeros((row_count, width_here), jnp.float32)
    for momentum_buffer in range(pieces + sections - 1):
        piece_index = momentum_buffer - section_index
        active = (piece_index >= 0) & (piece_index < pieces)
        row_start = jnp.clip(piece_index, 0, pieces - 1) * row_count
        first_rows = lax.dynamic_slice_in_dim(embedded, row_start, row_count, 0)
        hidden = jnp.where(section_index == 0, first_rows, incoming)
        moving = jnp.where(section_index == 0, jnp.zeros_like(incoming_move), incoming_move)
        onehot_rows = lax.dynamic_slice_in_dim(onehot, row_start, row_count, 0)
        for layer_index in range(layers_here):
            saved_hidden = keep_rows(saved_hidden, hidden, layer_index, row_start, active)
            hidden, moving, recip, lowrank = layer_forward(
                hidden,
                moving,
                onehot_rows,
                theta[layer_index],
                direction[layer_index],
                gains[layer_index],
            )
            saved_recip = keep_rows(saved_recip, recip, layer_index, row_start, active)
            saved_low = keep_rows(saved_low, lowrank, layer_index, row_start, active)
        final_move = keep_rows(final_move, moving, 0, row_start, active)
        incoming, incoming_move = shifted((hidden, moving), "section", 1)
    cot_output = final_move[0] * weights[:, None]
    gradient = jnp.zeros_like(theta)
    incoming_cot = jnp.zeros((row_count, width_here), jnp.float32)
    for momentum_buffer in range(pieces + sections - 1):
        piece_index = momentum_buffer - (sections - 1 - section_index)
        active = (piece_index >= 0) & (piece_index < pieces)
        row_start = jnp.clip(piece_index, 0, pieces - 1) * row_count
        last_rows = lax.dynamic_slice_in_dim(cot_output, row_start, row_count, 0)
        cotangent = jnp.where(section_index == sections - 1, last_rows, incoming_cot)
        onehot_rows = lax.dynamic_slice_in_dim(onehot, row_start, row_count, 0)
        for layer_index in reversed(range(layers_here)):
            hidden = lax.dynamic_slice_in_dim(saved_hidden[layer_index], row_start, row_count, 0)
            recip = lax.dynamic_slice_in_dim(saved_recip[layer_index], row_start, row_count, 0)
            lowrank = lax.dynamic_slice_in_dim(saved_low[layer_index], row_start, row_count, 0)
            cotangent, layer_grad = layer_backward(
                cotangent,
                hidden,
                recip,
                lowrank,
                onehot_rows,
                theta[layer_index],
                gains[layer_index],
            )
            gradient = gradient.at[layer_index].add(jnp.where(active, layer_grad, 0.0))
        incoming_cot = shifted(cotangent, "section", -1)
    product = gradient + DAMPING_FACTOR * direction
    curvature = lax.psum(jnp.sum(direction * product), ("section", "shard"))
    alpha = squared_old / curvature
    new_iterate = iterate + alpha * direction
    updated_residual_stream = residual - alpha * product
    squared_new = lax.psum(
        jnp.sum(updated_residual_stream * updated_residual_stream), ("section", "shard")
    )
    new_direction = updated_residual_stream + squared_new / squared_old * direction
    return (new_iterate, updated_residual_stream, new_direction)


def solution(mesh):
    return jax.shard_map(
        body,
        mesh=mesh,
        in_specs=(
            P("groups", "shard"),
            P("section", "shard"),
            P("section", "groups", None, None, "shard"),
            P("section", "groups", None, None, "shard"),
            P("section", "groups", None, None, "shard"),
            P("section", "groups", None, None, "shard"),
            P("groups"),
            P("groups"),
        ),
        out_specs=(
            P("section", "groups", None, None, "shard"),
            P("section", "groups", None, None, "shard"),
            P("section", "groups", None, None, "shard"),
        ),
        check_vma=False,
    )
```

profile of v0, /device:TPU:0, one launch (start us, length us, event | category | flops | bytes accessed | tf_op | source)
XLA Modules:
  0.0 1198.5 jit_solution(992745657408571423)
XLA Ops:
  19.2 18.1 %all-reduce.6 = (f32[256]{0:T(256)S(1)}, f32[256]{0:T(256)S(1)}) all-reduce(f32[256]{0:T(256)S(1)} %get-tuple-element.79, f32[256]{0:T(256)S(1)} %get-tuple-element.78), channel_id=1, replica_groups=mesh['groups'=2,'section'=2,'shard'=8] {'shard'}, use_global_device_ids=true, to_apply=%region_3.4 | all-reduce | flops 512 | bytes 4096 | tf_op jit(solution)/shard_map/psum | solution.py:48
  54.5 42.4 %all-reduce.48.cloned.1.call-done = (f32[256,64]{0,1:T(8,128)}, f32[256,64]{0,1:T(8,128)}) async-done(((f32[256,64]{0,1:T(8,128)}, f32[256,64]{0,1:T(8,128)}), (f32[256,64]{0,1:T(8,128)}, f32[256,64]{0,1:T(8,128)})) %all-reduce.48.cloned.1.call-update) | async-done | bytes 131088 | tf_op jit(solution)/shard_map/psum | solution.py:55
  102.3 13.9 %all-reduce.5 = (f32[256]{0:T(256)S(1)}, f32[256]{0:T(256)S(1)}) all-reduce(f32[256]{0:T(256)S(1)} %get-tuple-element.89, f32[256]{0:T(256)S(1)} %get-tuple-element.88), channel_id=1, replica_groups=mesh['groups'=2,'section'=2,'shard'=8] {'shard'}, use_global_device_ids=true, to_apply=%region_12.13 | all-reduce | flops 512 | bytes 4096 | tf_op jit(solution)/shard_map/psum | solution.py:48
  123.9 52.4 %all-reduce.46.cloned.1.call-done = (f32[256,64]{0,1:T(8,128)}, f32[256,64]{0,1:T(8,128)}) async-done(((f32[256,64]{0,1:T(8,128)}, f32[256,64]{0,1:T(8,128)}), (f32[256,64]{0,1:T(8,128)}, f32[256,64]{0,1:T(8,128)})) %all-reduce.46.cloned.1.call-update) | async-done | bytes 131088 | tf_op jit(solution)/shard_map/psum | solution.py:55
  189.0 17.4 %collective-permute-done.1 = f32[256,1024]{1,0:T(8,128)S(1)} collective-permute-done((f32[256,1024]{1,0:T(8,128)S(1)}, f32[256,1024]{1,0:T(8,128)S(1)}, u32[]{:S(2)}, u32[]{:S(2)}) %collective-permute-start.1) | collective-permute-done | bytes 1048608 | tf_op jit(solution)/shard_map/ppermute | solution.py:18
  207.7 18.4 %collective-permute-done = f32[256,1024]{1,0:T(8,128)S(1)} collective-permute-done((f32[256,1024]{1,0:T(8,128)S(1)}, f32[256,1024]{1,0:T(8,128)S(1)}, u32[]{:S(2)}, u32[]{:S(2)}) %collective-permute-start) | collective-permute-done | bytes 1048608 | tf_op jit(solution)/shard_map/ppermute | solution.py:18
  227.4 13.9 %all-reduce.4 = (f32[256]{0:T(256)S(1)}, f32[256]{0:T(256)S(1)}) all-reduce(f32[256]{0:T(256)S(1)} %get-tuple-element.87, f32[256]{0:T(256)S(1)} %get-tuple-element.86), channel_id=1, replica_groups=mesh['groups'=2,'section'=2,'shard'=8] {'shard'}, use_global_device_ids=true, to_apply=%region_21.22 | all-reduce | flops 512 | bytes 4096 | tf_op jit(solution)/shard_map/psum | solution.py:48
  250.5 54.8 %all-reduce.44.cloned.1.call-done = (f32[256,64]{0,1:T(8,128)}, f32[256,64]{0,1:T(8,128)}) async-done(((f32[256,64]{0,1:T(8,128)}, f32[256,64]{0,1:T(8,128)}), (f32[256,64]{0,1:T(8,128)}, f32[256,64]{0,1:T(8,128)})) %all-reduce.44.cloned.1.call-update) | async-done | bytes 131088 | tf_op jit(solution)/shard_map/psum | solution.py:55
  311.1 13.8 %all-reduce.3 = (f32[256]{0:T(256)S(1)}, f32[256]{0:T(256)S(1)}) all-reduce(f32[256]{0:T(256)S(1)} %get-tuple-element.85, f32[256]{0:T(256)S(1)} %get-tuple-element.84), channel_id=1, replica_groups=mesh['groups'=2,'section'=2,'shard'=8] {'shard'}, use_global_device_ids=true, to_apply=%region_30.31 | all-reduce | flops 512 | bytes 4096 | tf_op jit(solution)/shard_map/psum | solution.py:48
  335.0 53.5 %all-reduce.42.cloned.1.call-done = (f32[256,64]{0,1:T(8,128)}, f32[256,64]{0,1:T(8,128)}) async-done(((f32[256,64]{0,1:T(8,128)}, f32[256,64]{0,1:T(8,128)}), (f32[256,64]{0,1:T(8,128)}, f32[256,64]{0,1:T(8,128)})) %all-reduce.42.cloned.1.call-update) | async-done | bytes 131088 | tf_op jit(solution)/shard_map/psum | solution.py:55
  403.6 15.1 %collective-permute-done.3 = f32[256,1024]{1,0:T(8,128)S(1)} collective-permute-done((f32[256,1024]{1,0:T(8,128)S(1)}, f32[256,1024]{1,0:T(8,128)S(1)}, u32[]{:S(2)}, u32[]{:S(2)}) %collective-permute-start.3) | collective-permute-done | bytes 1048608 | tf_op jit(solution)/shard_map/ppermute | solution.py:18
  420.0 18.4 %collective-permute-done.2 = f32[256,1024]{1,0:T(8,128)S(1)} collective-permute-done((f32[256,1024]{1,0:T(8,128)S(1)}, f32[256,1024]{1,0:T(8,128)S(1)}, u32[]{:S(2)}, u32[]{:S(2)}) %collective-permute-start.2) | collective-permute-done | bytes 1048608 | tf_op jit(solution)/shard_map/ppermute | solution.py:18
  439.6 13.7 %all-reduce.2 = (f32[256]{0:T(256)S(1)}, f32[256]{0:T(256)S(1)}) all-reduce(f32[256]{0:T(256)S(1)} %get-tuple-element.83, f32[256]{0:T(256)S(1)} %get-tuple-element.82), channel_id=1, replica_groups=mesh['groups'=2,'section'=2,'shard'=8] {'shard'}, use_global_device_ids=true, to_apply=%region_39.40 | all-reduce | flops 512 | bytes 4096 | tf_op jit(solution)/shard_map/psum | solution.py:48
  463.7 53.8 %all-reduce.40.cloned.1.call-done = (f32[256,64]{0,1:T(8,128)}, f32[256,64]{0,1:T(8,128)}) async-done(((f32[256,64]{0,1:T(8,128)}, f32[256,64]{0,1:T(8,128)}), (f32[256,64]{0,1:T(8,128)}, f32[256,64]{0,1:T(8,128)})) %all-reduce.40.cloned.1.call-update) | async-done | bytes 131088 | tf_op jit(solution)/shard_map/psum | solution.py:55
  523.3 13.7 %all-reduce.1 = (f32[256]{0:T(256)S(1)}, f32[256]{0:T(256)S(1)}) all-reduce(f32[256]{0:T(256)S(1)} %get-tuple-element.81, f32[256]{0:T(256)S(1)} %get-tuple-element.80), channel_id=1, replica_groups=mesh['groups'=2,'section'=2,'shard'=8] {'shard'}, use_global_device_ids=true, to_apply=%region_48.49 | all-reduce | flops 512 | bytes 4096 | tf_op jit(solution)/shard_map/psum | solution.py:48
  554.4 53.3 %all-reduce.38.cloned.1.call-done = (f32[256,64]{0,1:T(8,128)}, f32[256,64]{0,1:T(8,128)}) async-done(((f32[256,64]{0,1:T(8,128)}, f32[256,64]{0,1:T(8,128)}), (f32[256,64]{0,1:T(8,128)}, f32[256,64]{0,1:T(8,128)})) %all-reduce.38.cloned.1.call-update) | async-done | bytes 131088 | tf_op jit(solution)/shard_map/psum | solution.py:55
  617.5 52.5 %all-reduce.26.cloned.1.call-done = f32[256,64]{0,1:T(8,128)} async-done(((f32[256,64]{0,1:T(8,128)}), f32[256,64]{0,1:T(8,128)}) %all-reduce.26.cloned.1.call-update) | async-done | bytes 65552 | tf_op jit(solution)/shard_map/psum | solution.py:79
  673.4 13.8 %psum.292 = f32[256]{0:T(256)S(1)} all-reduce(f32[256]{0:T(256)S(1)} %get-tuple-element.181), channel_id=1, replica_groups=mesh['groups'=2,'section'=2,'shard'=8] {'shard'}, use_global_device_ids=true, to_apply=%region_59.60 | all-reduce | flops 256 | bytes 2048 | tf_op jit(solution)/shard_map/psum | solution.py:83
  692.3 51.0 %all-reduce.28.cloned.1.call-done = f32[256,64]{0,1:T(8,128)} async-done(((f32[256,64]{0,1:T(8,128)}), f32[256,64]{0,1:T(8,128)}) %all-reduce.28.cloned.1.call-update) | async-done | bytes 65552 | tf_op jit(solution)/shard_map/psum | solution.py:79
  746.9 13.7 %psum.294 = f32[256]{0:T(256)S(1)} all-reduce(f32[256]{0:T(256)S(1)} %get-tuple-element.183), channel_id=1, replica_groups=mesh['groups'=2,'section'=2,'shard'=8] {'shard'}, use_global_device_ids=true, to_apply=%region_63.64 | all-reduce | flops 256 | bytes 2048 | tf_op jit(solution)/shard_map/psum | solution.py:83
  772.9 16.5 %collective-permute-done.4 = f32[256,1024]{1,0:T(8,128)S(1)} collective-permute-done((f32[256,1024]{1,0:T(8,128)S(1)}, f32[256,1024]{1,0:T(8,128)S(1)}, u32[]{:S(2)}, u32[]{:S(2)}) %collective-permute-start.4) | collective-permute-done | bytes 1048608 | tf_op jit(solution)/shard_map/ppermute | solution.py:18
  794.5 47.8 %all-reduce.30.cloned.1.call-done = f32[256,64]{0,1:T(8,128)} async-done(((f32[256,64]{0,1:T(8,128)}), f32[256,64]{0,1:T(8,128)}) %all-reduce.30.cloned.1.call-update) | async-done | bytes 65552 | tf_op jit(solution)/shard_map/psum | solution.py:79
  845.6 14.2 %psum.296 = f32[256]{0:T(256)S(1)} all-reduce(f32[256]{0:T(256)S(1)} %get-tuple-element.185), channel_id=1, replica_groups=mesh['groups'=2,'section'=2,'shard'=8] {'shard'}, use_global_device_ids=true, to_apply=%region_67.68 | all-reduce | flops 256 | bytes 2048 | tf_op jit(solution)/shard_map/psum | solution.py:83
  868.6 47.0 %all-reduce.32.cloned.1.call-done = f32[256,64]{0,1:T(8,128)} async-done(((f32[256,64]{0,1:T(8,128)}), f32[256,64]{0,1:T(8,128)}) %all-reduce.32.cloned.1.call-update) | async-done | bytes 65552 | tf_op jit(solution)/shard_map/psum | solution.py:79
  919.2 13.8 %psum.298 = f32[256]{0:T(256)S(1)} all-reduce(f32[256]{0:T(256)S(1)} %get-tuple-element.187), channel_id=1, replica_groups=mesh['groups'=2,'section'=2,'shard'=8] {'shard'}, use_global_device_ids=true, to_apply=%region_71.72 | all-reduce | flops 256 | bytes 2048 | tf_op jit(solution)/shard_map/psum | solution.py:83
  943.5 18.5 %collective-permute-done.5 = f32[256,1024]{1,0:T(8,128)S(1)} collective-permute-done((f32[256,1024]{1,0:T(8,128)S(1)}, f32[256,1024]{1,0:T(8,128)S(1)}, u32[]{:S(2)}, u32[]{:S(2)}) %collective-permute-start.5) | collective-permute-done | bytes 1048608 | tf_op jit(solution)/shard_map/ppermute | solution.py:18
  966.1 48.8 %all-reduce.34.cloned.1.call-done = f32[256,64]{0,1:T(8,128)} async-done(((f32[256,64]{0,1:T(8,128)}), f32[256,64]{0,1:T(8,128)}) %all-reduce.34.cloned.1.call-update) | async-done | bytes 65552 | tf_op jit(solution)/shard_map/psum | solution.py:79
  1018.2 13.7 %psum.300 = f32[256]{0:T(256)S(1)} all-reduce(f32[256]{0:T(256)S(1)} %get-tuple-element.189), channel_id=1, replica_groups=mesh['groups'=2,'section'=2,'shard'=8] {'shard'}, use_global_device_ids=true, to_apply=%region_75.76 | all-reduce | flops 256 | bytes 2048 | tf_op jit(solution)/shard_map/psum | solution.py:83
  1042.9 44.9 %all-reduce.36.cloned.1.call-done = f32[256,64]{0,1:T(8,128)} async-done(((f32[256,64]{0,1:T(8,128)}), f32[256,64]{0,1:T(8,128)}) %all-reduce.36.cloned.1.call-update) | async-done | bytes 65552 | tf_op jit(solution)/shard_map/psum | solution.py:79
  1097.2 31.2 %all-reduce = (f32[]{:T(128)}, f32[]{:T(128)}) all-reduce(f32[]{:T(128)} %multiply_reduce_fusion.2, f32[]{:T(128)} %multiply_reduce_fusion.1), channel_id=1, replica_groups=mesh['groups'=2,'section'=2,'shard'=8] {'section','shard'}, use_global_device_ids=true, to_apply=%region_1.0 | all-reduce | flops 2 | bytes 16 | tf_op jit(solution)/shard_map/psum | solution.py:93
  1129.7 9.5 multiply_reduce_fusion
  1139.3 30.3 %psum.303 = f32[]{:T(128)} all-reduce(f32[]{:T(128)} %get-tuple-element.116), channel_id=1, replica_groups=mesh['groups'=2,'section'=2,'shard'=8] {'section','shard'}, use_global_device_ids=true, to_apply=%region_81.82 | all-reduce | flops 1 | bytes 8 | tf_op jit(solution)/shard_map/psum | solution.py:165
  (360 shorter events, 246.2 us)
Async XLA Ops:
  7.2 89.6 %all-reduce.48.cloned.1.call-start = ((), (), s32[]{:S(2)}) async-start(), calls=%async_computation.11 | async-start | bytes 262144 | tf_op jit(solution)/shard_map/psum | solution.py:55
  16.9 25.1 %copy-start = (f32[1,4,2,64,1024]{4,3,1,2,0:T(8,128)}, f32[1,4,2,64,1024]{4,3,1,2,0:T(8,128)S(1)}, u32[]{:S(2)}) copy-start(f32[1,4,2,64,1024]{4,3,1,2,0:T(8,128)S(1)} %copy.39) | copy-start | bytes 6291460
  44.0 132.3 %all-reduce.46.cloned.1.call-start = ((), (), s32[]{:S(2)}) async-start(), calls=%async_computation.10 | async-start | bytes 262144 | tf_op jit(solution)/shard_map/psum | solution.py:55
  123.6 181.7 %all-reduce.44.cloned.1.call-start = ((), (), s32[]{:S(2)}) async-start(), calls=%async_computation.9 | async-start | bytes 262144 | tf_op jit(solution)/shard_map/psum | solution.py:55
  179.5 27.0 %collective-permute-start.1 = (f32[256,1024]{1,0:T(8,128)S(1)}, f32[256,1024]{1,0:T(8,128)S(1)}, u32[]{:S(2)}, u32[]{:S(2)}) collective-permute-start(f32[256,1024]{1,0:T(8,128)S(1)} %fusion.8), channel_id=1, source_target_pairs={{0,8},{1,9},{2,10},{3,11},{4,12},{5,13},{6,14},{7,15},{16,24},{17,... | collective-permute-start | bytes 3145736 | tf_op jit(solution)/shard_map/ppermute | solution.py:18
  184.4 41.7 %collective-permute-start = (f32[256,1024]{1,0:T(8,128)S(1)}, f32[256,1024]{1,0:T(8,128)S(1)}, u32[]{:S(2)}, u32[]{:S(2)}) collective-permute-start(f32[256,1024]{1,0:T(8,128)S(1)} %get-tuple-element.176), channel_id=1, source_target_pairs={{0,8},{1,9},{2,10},{3,11},{4,12},{5,13},{6,14},{7,15},{16,24},{17,... | collective-permute-start | bytes 3145736 | tf_op jit(solution)/shard_map/ppermute | solution.py:18
  185.8 20.7 %copy-start.19 = (f32[512,1024]{1,0:T(8,128)S(1)}, f32[512,1024]{1,0:T(8,128)}, u32[]{:S(2)}) copy-start(f32[512,1024]{1,0:T(8,128)} %convert_element_type.10) | copy-start | bytes 6291460
  250.3 138.2 %all-reduce.42.cloned.1.call-start = ((), (), s32[]{:S(2)}) async-start(), calls=%async_computation.8 | async-start | bytes 262144 | tf_op jit(solution)/shard_map/psum | solution.py:55
  311.1 17.3 %copy-start.24 = (f32[256,1024]{1,0:T(8,128)S(1)}, f32[256,1024]{1,0:T(8,128)}, u32[]{:S(2)}) copy-start(f32[256,1024]{1,0:T(8,128)} %get-tuple-element.177) | copy-start | bytes 3145732
  334.6 182.9 %all-reduce.40.cloned.1.call-start = ((), (), s32[]{:S(2)}) async-start(), calls=%async_computation.7 | async-start | bytes 262144 | tf_op jit(solution)/shard_map/psum | solution.py:55
  388.6 6.6 copy-start.34
  388.6 6.6 copy-start.46
  388.6 6.6 copy-start.74
  391.7 27.0 %collective-permute-start.3 = (f32[256,1024]{1,0:T(8,128)S(1)}, f32[256,1024]{1,0:T(8,128)S(1)}, u32[]{:S(2)}, u32[]{:S(2)}) collective-permute-start(f32[256,1024]{1,0:T(8,128)S(1)} %fusion.12), channel_id=1, source_target_pairs={{0,8},{1,9},{2,10},{3,11},{4,12},{5,13},{6,14},{7,15},{16,24},{17,... | collective-permute-start | bytes 3145736 | tf_op jit(solution)/shard_map/ppermute | solution.py:18
  397.8 40.6 %collective-permute-start.2 = (f32[256,1024]{1,0:T(8,128)S(1)}, f32[256,1024]{1,0:T(8,128)S(1)}, u32[]{:S(2)}, u32[]{:S(2)}) collective-permute-start(f32[256,1024]{1,0:T(8,128)S(1)} %get-tuple-element.179), channel_id=1, source_target_pairs={{0,8},{1,9},{2,10},{3,11},{4,12},{5,13},{6,14},{7,15},{16,24},{17,... | collective-permute-start | bytes 3145736 | tf_op jit(solution)/shard_map/ppermute | solution.py:18
  401.6 17.1 %copy-start.20 = (f32[512,1024]{1,0:T(8,128)S(1)}, f32[512,1024]{1,0:T(8,128)}, u32[]{:S(2)}) copy-start(f32[512,1024]{1,0:T(8,128)} %convert_element_type.10) | copy-start | bytes 6291460
  463.4 144.4 %all-reduce.38.cloned.1.call-start = ((), (), s32[]{:S(2)}) async-start(), calls=%async_computation.6 | async-start | bytes 262144 | tf_op jit(solution)/shard_map/psum | solution.py:55
  537.0 6.2 copy-start.29
  537.0 6.2 copy-start.60
  553.7 116.3 %all-reduce.26.cloned.1.call-start = ((), (), s32[]{:S(2)}) async-start(), calls=%async_computation | async-start | bytes 131072 | tf_op jit(solution)/shard_map/psum | solution.py:79
  617.2 126.0 %all-reduce.28.cloned.1.call-start = ((), (), s32[]{:S(2)}) async-start(), calls=%async_computation.1 | async-start | bytes 131072 | tf_op jit(solution)/shard_map/psum | solution.py:79
  691.4 150.9 %all-reduce.30.cloned.1.call-start = ((), (), s32[]{:S(2)}) async-start(), calls=%async_computation.2 | async-start | bytes 131072 | tf_op jit(solution)/shard_map/psum | solution.py:79
  762.6 26.8 %collective-permute-start.4 = (f32[256,1024]{1,0:T(8,128)S(1)}, f32[256,1024]{1,0:T(8,128)S(1)}, u32[]{:S(2)}, u32[]{:S(2)}) collective-permute-start(f32[256,1024]{1,0:T(8,128)S(1)} %fusion.105), channel_id=1, source_target_pairs={{8,0},{9,1},{10,2},{11,3},{12,4},{13,5},{14,6},{15,7},{24,16},{25,... | collective-permute-start | bytes 3145736 | tf_op jit(solution)/shard_map/ppermute | solution.py:18
  791.3 124.3 %all-reduce.32.cloned.1.call-start = ((), (), s32[]{:S(2)}) async-start(), calls=%async_computation.3 | async-start | bytes 131072 | tf_op jit(solution)/shard_map/psum | solution.py:79
  863.7 151.2 %all-reduce.34.cloned.1.call-start = ((), (), s32[]{:S(2)}) async-start(), calls=%async_computation.4 | async-start | bytes 131072 | tf_op jit(solution)/shard_map/psum | solution.py:79
  933.0 7.0 copy-start.50
  933.0 7.0 copy-start.54
  935.3 26.8 %collective-permute-start.5 = (f32[256,1024]{1,0:T(8,128)S(1)}, f32[256,1024]{1,0:T(8,128)S(1)}, u32[]{:S(2)}, u32[]{:S(2)}) collective-permute-start(f32[256,1024]{1,0:T(8,128)S(1)} %fusion.90), channel_id=1, source_target_pairs={{8,0},{9,1},{10,2},{11,3},{12,4},{13,5},{14,6},{15,7},{24,16},{25,... | collective-permute-start | bytes 3145736 | tf_op jit(solution)/shard_map/ppermute | solution.py:18
  942.8 19.3 %copy-start.32 = (f32[512,1024]{1,0:T(8,128)S(1)}, f32[512,1024]{1,0:T(8,128)}, u32[]{:S(2)}) copy-start(f32[512,1024]{1,0:T(8,128)} %copy-done.30) | copy-start | bytes 6291460
  943.5 19.7 %copy-start.11 = (f32[2,4,2,64,1024]{4,3,1,2,0:T(8,128)}, f32[2,4,2,64,1024]{4,3,1,2,0:T(8,128)S(1)}, u32[]{:S(2)}) copy-start(f32[2,4,2,64,1024]{4,3,1,2,0:T(8,128)S(1)} %fusion.2) | copy-start | bytes 12582916
  963.9 123.9 %all-reduce.36.cloned.1.call-start = ((), (), s32[]{:S(2)}) async-start(), calls=%async_computation.5 | async-start | bytes 131072 | tf_op jit(solution)/shard_map/psum | solution.py:79
  1041.9 46.0 %copy-start.23 = (f32[1,512,1024]{2,1,0:T(8,128)S(1)}, f32[1,512,1024]{2,1,0:T(8,128)}, u32[]{:S(2)}) copy-start(f32[1,512,1024]{2,1,0:T(8,128)} %get-tuple-element.124) | copy-start | bytes 6291460
  (68 other events, 192.0 us)
Sparse Core Ops, SparseCore 0:
  44.1 52.6 all-reduce.47
  123.7 52.5 all-reduce.45
  250.4 54.7 all-reduce.43
  334.7 53.8 all-reduce.41
  463.5 53.9 all-reduce.39
  553.9 53.8 all-reduce.37
  617.4 52.6 all-reduce.25
  691.5 51.7 all-reduce.27
  791.4 50.8 all-reduce.29
  863.8 51.7 all-reduce.31
  964.0 50.8 all-reduce.33
  1036.0 51.7 all-reduce.35
where the time goes:
time: 1210 us; the launch traced here: 1200 us
  waiting for transfers between devices  707 us (58%)
  blocking collectives  218 us (18%)
  matrix products  109 us (9%)
  other arithmetic  80.2 us (7%)
  local copies, waits for them, and re-layouts  52.5 us (4%)
  between operations  18.5 us (2%)
  starting transfers between devices  13.9 us (1%)
    psum x6, waiting for transfers between devices, layer_forward(): lax.psum((pick_down(normed, parameters[:, 0], onehot) * down_scale, (pick...  310 us
    psum x6, waiting for transfers between devices, layer_backward(): low_cot = lax.psum(partial_cot, 'shard')  292 us
    ppermute x6, waiting for transfers between devices, shifted(): lax.ppermute(value, axis, [(source, source + steps) for source in range(i...  104 us
    psum x6, blocking collectives, layer_forward(): lax.psum((jnp.sum(hidden * hidden, axis=-1), jnp.sum(hidden * moving, axi...  87.1 us
    psum x5, blocking collectives, layer_backward(): lax.psum(jnp.sum(cot_norm * gain_vector * hidden, axis=-1), 'shard')  69.1 us
    dot_general x22, matrix products, apply_up_projection(): return jnp.einsum('tkr,krd->td', picked, mats, precision=HIGH)  48.2 us
    dot_general x24, matrix products, pick_down(): expanded = jnp.einsum('td,krd->tkr', values, mats, precision=HIGH)  42.6 us
    psum x1, blocking collectives, body(): squared_old = lax.psum(jnp.sum(residual * residual), ('section', 'shard'))  31.2 us
  transfers between devices with their start and end apart: 18, of which 18 were waited for; matrix products, arithmetic and copies ran while one was open for 5% of the time, Pallas kernels for 0%

commit v1 on v0

--- a/solution.py
+++ b/solution.py
@@ -10,6 +10,10 @@
 ADAPTER_SCALE = 0.5
 DAMPING_FACTOR = 0.5
 HIGH = lax.Precision.HIGHEST
+
+
+def begin_terms(xin):
+    return jnp.sum(lax.all_gather(xin, "shard"), 0)
 
 
 def shifted(value, axis, steps):
@@ -76,7 +80,7 @@
     up_projection_scale = ADAPTER_SCALE * ADAPTER_RANK ** (-0.5)
     grad_up = up_projection_scale * task_outer(lowrank, cotangent, onehot)
     partial_cot = up_projection_scale * pick_down(cotangent, parameters[:, 1], onehot)
-    low_cot = lax.psum(partial_cot, "shard")
+    low_cot = begin_terms(partial_cot)
     normed = hidden * gain_vector * recip[:, None]
     grad_down = down_scale * task_outer(low_cot, normed, onehot)
     cot_norm = down_scale * apply_up_projection(low_cot, parameters[:, 0], onehot)

time: 1210 us -> 984 us (0.81)
  waiting for transfers between devices: 707 us -> 414 us
  blocking collectives: 218 us -> 310 us
  other arithmetic: 80.2 us -> 63.5 us
    psum x6 -> x0, waiting for transfers between devices: 292 us -> none  [layer_backward(): low_cot = lax.psum(partial_cot, 'shard')]
    all_gather x0 -> x6, blocking collectives: none -> 90.3 us  [begin_terms(): return jnp.sum(lax.all_gather(xin, 'shard'), 0)]
    unnamed x170 -> x204, local copies, waits for them, and re-layouts: 23.6 us -> 24.6 us
  transfers between devices with their start and end apart: 18 -> 12, of which waited for: 18 -> 12; matrix products, arithmetic and copies ran while one was open for 5% -> 4% of each run, Pallas kernels for 0% -> 0%
where the time goes in v1:
time: 984 us; the launch traced here: 975 us
  waiting for transfers between devices  414 us (42%)
  blocking collectives  310 us (32%)
  matrix products  99 us (10%)
  other arithmetic  63.5 us (6%)
  local copies, waits for them, and re-layouts  56 us (6%)
  between operations  18.8 us (2%)
  starting transfers between devices  13.5 us (1%)
    psum x6, waiting for transfers between devices, layer_forward(): lax.psum((pick_down(normed, parameters[:, 0], onehot) * down_scale, (pick...  309 us
    ppermute x6, waiting for transfers between devices, shifted(): lax.ppermute(value, axis, [(source, source + steps) for source in range(i...  105 us
    all_gather x6, blocking collectives, begin_terms(): return jnp.sum(lax.all_gather(xin, 'shard'), 0)  90.3 us
    psum x6, blocking collectives, layer_forward(): lax.psum((jnp.sum(hidden * hidden, axis=-1), jnp.sum(hidden * moving, axi...  87.5 us
    psum x5, blocking collectives, layer_backward(): lax.psum(jnp.sum(cot_norm * gain_vector * hidden, axis=-1), 'shard')  71.6 us
    dot_general x24, matrix products, pick_down(): expanded = jnp.einsum('td,krd->tkr', values, mats, precision=HIGH)  42.5 us
    dot_general x22, matrix products, apply_up_projection(): return jnp.einsum('tkr,krd->td', picked, mats, precision=HIGH)  42 us
    psum x1, blocking collectives, body(): squared_old = lax.psum(jnp.sum(residual * residual), ('section', 'shard'))  30.4 us
  transfers between devices with their start and end apart: 12, of which 12 were waited for; matrix products, arithmetic and copies ran while one was open for 4% of the time, Pallas kernels for 0%

profile of v1, /device:TPU:0, one launch (start us, length us, event | category | flops | bytes accessed | tf_op | source)
XLA Modules:
  0.0 974.9 jit_solution(11028555463367784960)
XLA Ops:
  19.2 18.1 %all-reduce.6 = (f32[256]{0:T(256)S(1)}, f32[256]{0:T(256)S(1)}) all-reduce(f32[256]{0:T(256)S(1)} %get-tuple-element.82, f32[256]{0:T(256)S(1)} %get-tuple-element.81), channel_id=1, replica_groups=mesh['groups'=2,'section'=2,'shard'=8] {'shard'}, use_global_device_ids=true, to_apply=%region_3.4 | all-reduce | flops 512 | bytes 4096 | tf_op jit(solution)/shard_map/psum | solution.py:52
  56.0 41.2 %all-reduce.30.cloned.1.call-done = (f32[256,64]{0,1:T(8,128)}, f32[256,64]{0,1:T(8,128)}) async-done(((f32[256,64]{0,1:T(8,128)}, f32[256,64]{0,1:T(8,128)}), (f32[256,64]{0,1:T(8,128)}, f32[256,64]{0,1:T(8,128)})) %all-reduce.30.cloned.1.call-update) | async-done | bytes 131088 | tf_op jit(solution)/shard_map/psum | solution.py:59
  102.6 14.2 %all-reduce.5 = (f32[256]{0:T(256)S(1)}, f32[256]{0:T(256)S(1)}) all-reduce(f32[256]{0:T(256)S(1)} %get-tuple-element.92, f32[256]{0:T(256)S(1)} %get-tuple-element.91), channel_id=1, replica_groups=mesh['groups'=2,'section'=2,'shard'=8] {'shard'}, use_global_device_ids=true, to_apply=%region_12.13 | all-reduce | flops 512 | bytes 4096 | tf_op jit(solution)/shard_map/psum | solution.py:52
  124.6 52.4 %all-reduce.28.cloned.1.call-done = (f32[256,64]{0,1:T(8,128)}, f32[256,64]{0,1:T(8,128)}) async-done(((f32[256,64]{0,1:T(8,128)}, f32[256,64]{0,1:T(8,128)}), (f32[256,64]{0,1:T(8,128)}, f32[256,64]{0,1:T(8,128)})) %all-reduce.28.cloned.1.call-update) | async-done | bytes 131088 | tf_op jit(solution)/shard_map/psum | solution.py:59
  189.8 17.4 %collective-permute-done.1 = f32[256,1024]{1,0:T(8,128)S(1)} collective-permute-done((f32[256,1024]{1,0:T(8,128)S(1)}, f32[256,1024]{1,0:T(8,128)S(1)}, u32[]{:S(2)}, u32[]{:S(2)}) %collective-permute-start.1) | collective-permute-done | bytes 1048608 | tf_op jit(solution)/shard_map/ppermute | solution.py:22
  208.4 18.4 %collective-permute-done = f32[256,1024]{1,0:T(8,128)S(1)} collective-permute-done((f32[256,1024]{1,0:T(8,128)S(1)}, f32[256,1024]{1,0:T(8,128)S(1)}, u32[]{:S(2)}, u32[]{:S(2)}) %collective-permute-start) | collective-permute-done | bytes 1048608 | tf_op jit(solution)/shard_map/ppermute | solution.py:22
  228.2 13.9 %all-reduce.4 = (f32[256]{0:T(256)S(1)}, f32[256]{0:T(256)S(1)}) all-reduce(f32[256]{0:T(256)S(1)} %get-tuple-element.90, f32[256]{0:T(256)S(1)} %get-tuple-element.89), channel_id=1, replica_groups=mesh['groups'=2,'section'=2,'shard'=8] {'shard'}, use_global_device_ids=true, to_apply=%region_21.22 | all-reduce | flops 512 | bytes 4096 | tf_op jit(solution)/shard_map/psum | solution.py:52
  251.1 54.8 %all-reduce.26.cloned.1.call-done = (f32[256,64]{0,1:T(8,128)}, f32[256,64]{0,1:T(8,128)}) async-done(((f32[256,64]{0,1:T(8,128)}, f32[256,64]{0,1:T(8,128)}), (f32[256,64]{0,1:T(8,128)}, f32[256,64]{0,1:T(8,128)})) %all-reduce.26.cloned.1.call-update) | async-done | bytes 131088 | tf_op jit(solution)/shard_map/psum | solution.py:59
  311.8 13.8 %all-reduce.3 = (f32[256]{0:T(256)S(1)}, f32[256]{0:T(256)S(1)}) all-reduce(f32[256]{0:T(256)S(1)} %get-tuple-element.88, f32[256]{0:T(256)S(1)} %get-tuple-element.87), channel_id=1, replica_groups=mesh['groups'=2,'section'=2,'shard'=8] {'shard'}, use_global_device_ids=true, to_apply=%region_30.31 | all-reduce | flops 512 | bytes 4096 | tf_op jit(solution)/shard_map/psum | solution.py:52
  335.6 53.7 %all-reduce.24.cloned.1.call-done = (f32[256,64]{0,1:T(8,128)}, f32[256,64]{0,1:T(8,128)}) async-done(((f32[256,64]{0,1:T(8,128)}, f32[256,64]{0,1:T(8,128)}), (f32[256,64]{0,1:T(8,128)}, f32[256,64]{0,1:T(8,128)})) %all-reduce.24.cloned.1.call-update) | async-done | bytes 131088 | tf_op jit(solution)/shard_map/psum | solution.py:59
  404.3 15.1 %collective-permute-done.3 = f32[256,1024]{1,0:T(8,128)S(1)} collective-permute-done((f32[256,1024]{1,0:T(8,128)S(1)}, f32[256,1024]{1,0:T(8,128)S(1)}, u32[]{:S(2)}, u32[]{:S(2)}) %collective-permute-start.3) | collective-permute-done | bytes 1048608 | tf_op jit(solution)/shard_map/ppermute | solution.py:22
  420.7 18.4 %collective-permute-done.2 = f32[256,1024]{1,0:T(8,128)S(1)} collective-permute-done((f32[256,1024]{1,0:T(8,128)S(1)}, f32[256,1024]{1,0:T(8,128)S(1)}, u32[]{:S(2)}, u32[]{:S(2)}) %collective-permute-start.2) | collective-permute-done | bytes 1048608 | tf_op jit(solution)/shard_map/ppermute | solution.py:22
  440.3 13.7 %all-reduce.2 = (f32[256]{0:T(256)S(1)}, f32[256]{0:T(256)S(1)}) all-reduce(f32[256]{0:T(256)S(1)} %get-tuple-element.86, f32[256]{0:T(256)S(1)} %get-tuple-element.85), channel_id=1, replica_groups=mesh['groups'=2,'section'=2,'shard'=8] {'shard'}, use_global_device_ids=true, to_apply=%region_39.40 | all-reduce | flops 512 | bytes 4096 | tf_op jit(solution)/shard_map/psum | solution.py:52
  464.7 53.5 %all-reduce.22.cloned.1.call-done = (f32[256,64]{0,1:T(8,128)}, f32[256,64]{0,1:T(8,128)}) async-done(((f32[256,64]{0,1:T(8,128)}, f32[256,64]{0,1:T(8,128)}), (f32[256,64]{0,1:T(8,128)}, f32[256,64]{0,1:T(8,128)})) %all-reduce.22.cloned.1.call-update) | async-done | bytes 131088 | tf_op jit(solution)/shard_map/psum | solution.py:59
  524.0 13.7 %all-reduce.1 = (f32[256]{0:T(256)S(1)}, f32[256]{0:T(256)S(1)}) all-reduce(f32[256]{0:T(256)S(1)} %get-tuple-element.84, f32[256]{0:T(256)S(1)} %get-tuple-element.83), channel_id=1, replica_groups=mesh['groups'=2,'section'=2,'shard'=8] {'shard'}, use_global_device_ids=true, to_apply=%region_48.49 | all-reduce | flops 512 | bytes 4096 | tf_op jit(solution)/shard_map/psum | solution.py:52
  555.7 53.4 %all-reduce.20.cloned.1.call-done = (f32[256,64]{0,1:T(8,128)}, f32[256,64]{0,1:T(8,128)}) async-done(((f32[256,64]{0,1:T(8,128)}, f32[256,64]{0,1:T(8,128)}), (f32[256,64]{0,1:T(8,128)}, f32[256,64]{0,1:T(8,128)})) %all-reduce.20.cloned.1.call-update) | async-done | bytes 131088 | tf_op jit(solution)/shard_map/psum | solution.py:59
  616.6 15.2 %all-gather = f32[2048,64]{0,1:T(8,128)S(1)} all-gather(f32[256,64]{0,1:T(8,128)S(1)} %broadcast_multiply_fusion.6), channel_id=2, replica_groups=mesh['groups'=2,'section'=2,'shard'=8] {'shard'}, dimensions={0}, use_global_device_ids=true | all-gather | bytes 589824 | tf_op jit(solution)/shard_map/all_gather | solution.py:16
  634.2 15.0 %psum.249 = f32[256]{0:T(256)S(1)} all-reduce(f32[256]{0:T(256)S(1)} %get-tuple-element.184), channel_id=1, replica_groups=mesh['groups'=2,'section'=2,'shard'=8] {'shard'}, use_global_device_ids=true, to_apply=%region_59.60 | all-reduce | flops 256 | bytes 2048 | tf_op jit(solution)/shard_map/psum | solution.py:87
  652.9 15.0 %all-gather.1 = f32[2048,64]{0,1:T(8,128)S(1)} all-gather(f32[256,64]{0,1:T(8,128)S(1)} %broadcast_multiply_fusion.5), channel_id=3, replica_groups=mesh['groups'=2,'section'=2,'shard'=8] {'shard'}, dimensions={0}, use_global_device_ids=true | all-gather | bytes 589824 | tf_op jit(solution)/shard_map/all_gather | solution.py:16
  670.9 14.6 %psum.250 = f32[256]{0:T(256)} all-reduce(f32[256]{0:T(256)} %get-tuple-element.186), channel_id=1, replica_groups=mesh['groups'=2,'section'=2,'shard'=8] {'shard'}, use_global_device_ids=true, to_apply=%region_63.64 | all-reduce | flops 256 | bytes 2048 | tf_op jit(solution)/shard_map/psum | solution.py:87
  698.4 16.4 %collective-permute-done.4 = f32[256,1024]{1,0:T(8,128)S(1)} collective-permute-done((f32[256,1024]{1,0:T(8,128)S(1)}, f32[256,1024]{1,0:T(8,128)S(1)}, u32[]{:S(2)}, u32[]{:S(2)}) %collective-permute-start.4) | collective-permute-done | bytes 1048608 | tf_op jit(solution)/shard_map/ppermute | solution.py:22
  716.0 14.9 %all-gather.2 = f32[2048,64]{0,1:T(8,128)S(1)} all-gather(f32[256,64]{0,1:T(8,128)S(1)} %broadcast_multiply_fusion.4), channel_id=4, replica_groups=mesh['groups'=2,'section'=2,'shard'=8] {'shard'}, dimensions={0}, use_global_device_ids=true | all-gather | bytes 589824 | tf_op jit(solution)/shard_map/all_gather | solution.py:16
  733.3 14.0 %psum.251 = f32[256]{0:T(256)S(1)} all-reduce(f32[256]{0:T(256)S(1)} %get-tuple-element.188), channel_id=1, replica_groups=mesh['groups'=2,'section'=2,'shard'=8] {'shard'}, use_global_device_ids=true, to_apply=%region_67.68 | all-reduce | flops 256 | bytes 2048 | tf_op jit(solution)/shard_map/psum | solution.py:87
  750.5 15.4 %all-gather.3 = f32[2048,64]{0,1:T(8,128)S(1)} all-gather(f32[256,64]{0,1:T(8,128)S(1)} %broadcast_multiply_fusion.3), channel_id=5, replica_groups=mesh['groups'=2,'section'=2,'shard'=8] {'shard'}, dimensions={0}, use_global_device_ids=true | all-gather | bytes 589824 | tf_op jit(solution)/shard_map/all_gather | solution.py:16
  768.4 13.9 %psum.252 = f32[256]{0:T(256)S(1)} all-reduce(f32[256]{0:T(256)S(1)} %get-tuple-element.190), channel_id=1, replica_groups=mesh['groups'=2,'section'=2,'shard'=8] {'shard'}, use_global_device_ids=true, to_apply=%region_71.72 | all-reduce | flops 256 | bytes 2048 | tf_op jit(solution)/shard_map/psum | solution.py:87
  792.3 19.2 %collective-permute-done.5 = f32[256,1024]{1,0:T(8,128)S(1)} collective-permute-done((f32[256,1024]{1,0:T(8,128)S(1)}, f32[256,1024]{1,0:T(8,128)S(1)}, u32[]{:S(2)}, u32[]{:S(2)}) %collective-permute-start.5) | collective-permute-done | bytes 1048608 | tf_op jit(solution)/shard_map/ppermute | solution.py:22
  812.6 14.9 %all-gather.4 = f32[2048,64]{0,1:T(8,128)S(1)} all-gather(f32[256,64]{0,1:T(8,128)S(1)} %broadcast_multiply_fusion.2), channel_id=6, replica_groups=mesh['groups'=2,'section'=2,'shard'=8] {'shard'}, dimensions={0}, use_global_device_ids=true | all-gather | bytes 589824 | tf_op jit(solution)/shard_map/all_gather | solution.py:16
  829.9 14.1 %psum.253 = f32[256]{0:T(256)S(1)} all-reduce(f32[256]{0:T(256)S(1)} %get-tuple-element.192), channel_id=1, replica_groups=mesh['groups'=2,'section'=2,'shard'=8] {'shard'}, use_global_device_ids=true, to_apply=%region_75.76 | all-reduce | flops 256 | bytes 2048 | tf_op jit(solution)/shard_map/psum | solution.py:87
  849.5 15.0 %all-gather.5 = f32[2048,64]{0,1:T(8,128)S(1)} all-gather(f32[256,64]{0,1:T(8,128)S(1)} %broadcast_multiply_fusion.1), channel_id=7, replica_groups=mesh['groups'=2,'section'=2,'shard'=8] {'shard'}, dimensions={0}, use_global_device_ids=true | all-gather | bytes 589824 | tf_op jit(solution)/shard_map/all_gather | solution.py:16
  874.3 30.4 %all-reduce = (f32[]{:T(128)}, f32[]{:T(128)}) all-reduce(f32[]{:T(128)} %multiply_reduce_fusion.2, f32[]{:T(128)} %multiply_reduce_fusion.1), channel_id=1, replica_groups=mesh['groups'=2,'section'=2,'shard'=8] {'section','shard'}, use_global_device_ids=true, to_apply=%region_1.0 | all-reduce | flops 2 | bytes 16 | tf_op jit(solution)/shard_map/psum | solution.py:97
  906.1 9.5 multiply_reduce_fusion
  915.6 30.3 %psum.255 = f32[]{:T(128)} all-reduce(f32[]{:T(128)} %get-tuple-element.119), channel_id=1, replica_groups=mesh['groups'=2,'section'=2,'shard'=8] {'section','shard'}, use_global_device_ids=true, to_apply=%region_81.82 | all-reduce | flops 1 | bytes 8 | tf_op jit(solution)/shard_map/psum | solution.py:169
  (388 shorter events, 222.6 us)
Async XLA Ops:
  7.2 90.0 %all-reduce.30.cloned.1.call-start = ((), (), s32[]{:S(2)}) async-start(), calls=%async_computation.5 | async-start | bytes 262144 | tf_op jit(solution)/shard_map/psum | solution.py:59
  16.9 25.6 %copy-start = (f32[1,4,2,64,1024]{4,3,1,2,0:T(8,128)}, f32[1,4,2,64,1024]{4,3,1,2,0:T(8,128)S(1)}, u32[]{:S(2)}) copy-start(f32[1,4,2,64,1024]{4,3,1,2,0:T(8,128)S(1)} %copy.58) | copy-start | bytes 6291460
  44.5 132.6 %all-reduce.28.cloned.1.call-start = ((), (), s32[]{:S(2)}) async-start(), calls=%async_computation.4 | async-start | bytes 262144 | tf_op jit(solution)/shard_map/psum | solution.py:59
  124.3 181.7 %all-reduce.26.cloned.1.call-start = ((), (), s32[]{:S(2)}) async-start(), calls=%async_computation.3 | async-start | bytes 262144 | tf_op jit(solution)/shard_map/psum | solution.py:59
  180.2 27.0 %collective-permute-start.1 = (f32[256,1024]{1,0:T(8,128)S(1)}, f32[256,1024]{1,0:T(8,128)S(1)}, u32[]{:S(2)}, u32[]{:S(2)}) collective-permute-start(f32[256,1024]{1,0:T(8,128)S(1)} %fusion.8), channel_id=1, source_target_pairs={{0,8},{1,9},{2,10},{3,11},{4,12},{5,13},{6,14},{7,15},{16,24},{17,... | collective-permute-start | bytes 3145736 | tf_op jit(solution)/shard_map/ppermute | solution.py:22
  185.1 41.7 %collective-permute-start = (f32[256,1024]{1,0:T(8,128)S(1)}, f32[256,1024]{1,0:T(8,128)S(1)}, u32[]{:S(2)}, u32[]{:S(2)}) collective-permute-start(f32[256,1024]{1,0:T(8,128)S(1)} %get-tuple-element.179), channel_id=1, source_target_pairs={{0,8},{1,9},{2,10},{3,11},{4,12},{5,13},{6,14},{7,15},{16,24},{17,... | collective-permute-start | bytes 3145736 | tf_op jit(solution)/shard_map/ppermute | solution.py:22
  186.5 20.7 %copy-start.22 = (f32[512,1024]{1,0:T(8,128)S(1)}, f32[512,1024]{1,0:T(8,128)}, u32[]{:S(2)}) copy-start(f32[512,1024]{1,0:T(8,128)} %convert_element_type.10) | copy-start | bytes 6291460
  251.0 138.3 %all-reduce.24.cloned.1.call-start = ((), (), s32[]{:S(2)}) async-start(), calls=%async_computation.2 | async-start | bytes 262144 | tf_op jit(solution)/shard_map/psum | solution.py:59
  311.8 17.3 %copy-start.29 = (f32[256,1024]{1,0:T(8,128)S(1)}, f32[256,1024]{1,0:T(8,128)}, u32[]{:S(2)}) copy-start(f32[256,1024]{1,0:T(8,128)} %get-tuple-element.180) | copy-start | bytes 3145732
  335.3 182.8 %all-reduce.22.cloned.1.call-start = ((), (), s32[]{:S(2)}) async-start(), calls=%async_computation.1 | async-start | bytes 262144 | tf_op jit(solution)/shard_map/psum | solution.py:59
  392.5 27.0 %collective-permute-start.3 = (f32[256,1024]{1,0:T(8,128)S(1)}, f32[256,1024]{1,0:T(8,128)S(1)}, u32[]{:S(2)}, u32[]{:S(2)}) collective-permute-start(f32[256,1024]{1,0:T(8,128)S(1)} %fusion.12), channel_id=1, source_target_pairs={{0,8},{1,9},{2,10},{3,11},{4,12},{5,13},{6,14},{7,15},{16,24},{17,... | collective-permute-start | bytes 3145736 | tf_op jit(solution)/shard_map/ppermute | solution.py:22
  398.5 40.6 %collective-permute-start.2 = (f32[256,1024]{1,0:T(8,128)S(1)}, f32[256,1024]{1,0:T(8,128)S(1)}, u32[]{:S(2)}, u32[]{:S(2)}) collective-permute-start(f32[256,1024]{1,0:T(8,128)S(1)} %get-tuple-element.182), channel_id=1, source_target_pairs={{0,8},{1,9},{2,10},{3,11},{4,12},{5,13},{6,14},{7,15},{16,24},{17,... | collective-permute-start | bytes 3145736 | tf_op jit(solution)/shard_map/ppermute | solution.py:22
  402.3 17.1 %copy-start.23 = (f32[512,1024]{1,0:T(8,128)S(1)}, f32[512,1024]{1,0:T(8,128)}, u32[]{:S(2)}) copy-start(f32[512,1024]{1,0:T(8,128)} %convert_element_type.10) | copy-start | bytes 6291460
  464.1 145.0 %all-reduce.20.cloned.1.call-start = ((), (), s32[]{:S(2)}) async-start(), calls=%async_computation | async-start | bytes 262144 | tf_op jit(solution)/shard_map/psum | solution.py:59
  615.5 16.6 %copy-start.35 = (f32[512,1024]{1,0:T(8,128)}, f32[512,1024]{1,0:T(8,128)S(1)}, u32[]{:S(2)}) copy-start(f32[512,1024]{1,0:T(8,128)S(1)} %broadcast_multiply_fusion) | copy-start | bytes 6291460
  615.5 16.6 %copy-start.16 = (f32[1,512,1024]{2,1,0:T(8,128)S(1)}, f32[1,512,1024]{2,1,0:T(8,128)}, u32[]{:S(2)}) copy-start(f32[1,512,1024]{2,1,0:T(8,128)} %get-tuple-element.128) | copy-start | bytes 6291460
  615.5 16.6 %copy-start.79 = (f32[1024]{0:T(1024)S(1)}, f32[1024]{0:T(1024)}, u32[]{:S(2)}) copy-start(f32[1024]{0:T(1024)} %broadcast_multiply_fusion.14) | copy-start | bytes 12292
  632.0 17.3 %copy-start.86 = (f32[1,256]{1,0:T(1,128)S(1)}, f32[1,256]{1,0:T(1,128)}, u32[]{:S(2)}) copy-start(f32[1,256]{1,0:T(1,128)} %get-tuple-element.194) | copy-start | bytes 3076
  651.8 16.4 %copy-start.24 = (f32[1,512,1024]{2,1,0:T(8,128)S(1)}, f32[1,512,1024]{2,1,0:T(8,128)}, u32[]{:S(2)}) copy-start(f32[1,512,1024]{2,1,0:T(8,128)} %get-tuple-element.127) | copy-start | bytes 6291460
  651.8 16.4 %copy-start.84 = (f32[1024]{0:T(1024)S(1)}, f32[1024]{0:T(1024)}, u32[]{:S(2)}) copy-start(f32[1024]{0:T(1024)} %broadcast_multiply_fusion.13) | copy-start | bytes 12292
  688.1 26.6 %collective-permute-start.4 = (f32[256,1024]{1,0:T(8,128)S(1)}, f32[256,1024]{1,0:T(8,128)S(1)}, u32[]{:S(2)}, u32[]{:S(2)}) collective-permute-start(f32[256,1024]{1,0:T(8,128)S(1)} %fusion.105), channel_id=1, source_target_pairs={{8,0},{9,1},{10,2},{11,3},{12,4},{13,5},{14,6},{15,7},{24,16},{25,... | collective-permute-start | bytes 3145736 | tf_op jit(solution)/shard_map/ppermute | solution.py:22
  714.9 16.2 %copy-start.80 = (f32[1024]{0:T(1024)S(1)}, f32[1024]{0:T(1024)}, u32[]{:S(2)}) copy-start(f32[1024]{0:T(1024)} %broadcast_multiply_fusion.14) | copy-start | bytes 12292
  749.4 16.8 %copy-start.52 = (f32[256,1024]{1,0:T(8,128)}, f32[256,1024]{1,0:T(8,128)S(1)}, u32[]{:S(2)}) copy-start(f32[256,1024]{1,0:T(8,128)S(1)} %fusion.97) | copy-start | bytes 3145732
  749.4 16.8 %copy-start.26 = (f32[1,512,1024]{2,1,0:T(8,128)S(1)}, f32[1,512,1024]{2,1,0:T(8,128)}, u32[]{:S(2)}) copy-start(f32[1,512,1024]{2,1,0:T(8,128)} %get-tuple-element.127) | copy-start | bytes 6291460
  749.4 16.8 %copy-start.85 = (f32[1024]{0:T(1024)S(1)}, f32[1024]{0:T(1024)}, u32[]{:S(2)}) copy-start(f32[1024]{0:T(1024)} %broadcast_multiply_fusion.13) | copy-start | bytes 12292
  766.1 16.3 %copy-start.90 = (f32[1,256]{1,0:T(1,128)S(1)}, f32[1,256]{1,0:T(1,128)}, u32[]{:S(2)}) copy-start(f32[1,256]{1,0:T(1,128)} %get-tuple-element.152) | copy-start | bytes 3076
  784.7 26.7 %collective-permute-start.5 = (f32[256,1024]{1,0:T(8,128)S(1)}, f32[256,1024]{1,0:T(8,128)S(1)}, u32[]{:S(2)}, u32[]{:S(2)}) collective-permute-start(f32[256,1024]{1,0:T(8,128)S(1)} %fusion.90), channel_id=1, source_target_pairs={{8,0},{9,1},{10,2},{11,3},{12,4},{13,5},{14,6},{15,7},{24,16},{25,... | collective-permute-start | bytes 3145736 | tf_op jit(solution)/shard_map/ppermute | solution.py:22
  791.5 19.9 %copy-start.37 = (f32[512,1024]{1,0:T(8,128)S(1)}, f32[512,1024]{1,0:T(8,128)}, u32[]{:S(2)}) copy-start(f32[512,1024]{1,0:T(8,128)} %copy-done.35) | copy-start | bytes 6291460
  792.2 37.7 %copy-start.11 = (f32[2,4,2,64,1024]{4,3,1,2,0:T(8,128)}, f32[2,4,2,64,1024]{4,3,1,2,0:T(8,128)S(1)}, u32[]{:S(2)}) copy-start(f32[2,4,2,64,1024]{4,3,1,2,0:T(8,128)S(1)} %fusion.2) | copy-start | bytes 12582916
  792.2 19.3 %copy-start.70 = (f32[256,4]{0,1:T(4,128)S(1)}, f32[256,4]{0,1:T(4,128)}, u32[]{:S(2)}) copy-start(f32[256,4]{0,1:T(4,128)} %get-tuple-element.141) | copy-start | bytes 12292
  827.7 16.4 %copy-start.88 = (f32[1,256]{1,0:T(1,128)S(1)}, f32[1,256]{1,0:T(1,128)}, u32[]{:S(2)}) copy-start(f32[1,256]{1,0:T(1,128)} %get-tuple-element.196) | copy-start | bytes 3076
  848.4 16.4 %copy-start.73 = (f32[256,64]{0,1:T(8,128)S(1)}, f32[256,64]{0,1:T(8,128)}, u32[]{:S(2)}) copy-start(f32[256,64]{0,1:T(8,128)} %get-tuple-element.135) | copy-start | bytes 196612
  (76 other events, 262.9 us)
Sparse Core Ops, SparseCore 0:
  44.6 52.5 all-reduce.29
  124.4 52.5 all-reduce.27
  251.1 54.7 all-reduce.25
  335.4 53.8 all-reduce.23
  464.2 53.8 all-reduce.21
  555.2 53.8 all-reduce.19
